TPU v7x, 512 devices: a whole 4x4x16 slice. The times are simulated.
512 devices in a mesh: row: 16 (over z), col: 8 (over x, y_hi), depth: 4 (over y_lo, core).
Axes of the slice: x: 4, y: 4 (y_hi: 2, y_lo: 2; y = y_hi * 2 + y_lo), z: 16, core: 2. Of those that a mesh axis runs over, the one named last changes fastest.
Arguments:
- a_vals: bfloat16 [16, 4, 8, 4, 128, 128], P('row', 'depth', 'col'), may hold values from 0.02 to 14.4, as said below
- a_rows: int32 [16, 4, 8, 4], P('row', 'depth', 'col'), may hold values from 0 to 1, as said below
- a_cols: int32 [16, 4, 8, 4], P('row', 'depth', 'col'), may hold values from 0 to 31, as said below
- a_count: int32 [16, 4, 8], P('row', 'depth', 'col'), may hold values from 1 to 4, as said below
- b_vals: bfloat16 [4, 16, 8, 12, 128, 128], P('depth', 'row', 'col'), may hold values from 0.019897461 to 0.5
- b_rows: int32 [4, 16, 8, 12], P('depth', 'row', 'col'), may hold values from 0 to 15, as said below
- b_cols: int32 [4, 16, 8, 12], P('depth', 'row', 'col'), may hold values from 0 to 7, as said below
- b_count: int32 [4, 16, 8], P('depth', 'row', 'col'), may hold values from 1 to 12, as said below
- keep: int32 [32, 8192], P('row', ('col', 'depth')), may hold values 0 or 1
Outputs:
- flow: float32 [4096, 8192], P('row', ('col', 'depth'))
Inputs may be any that keep to these rules, and one draw needn't show every extreme that they name: a_rows and a_cols name the block position of each slot of a left tile; the 4 slots of a tile, padding included, hold distinct positions. `a_cols`: see a_rows. `a_count`: live slots of a left tile; some tile is full. b_rows and b_cols name the block position of each slot of a right tile; the 12 slots of a tile, padding included, hold distinct positions. `b_cols`: see b_rows. `b_count`: live slots of a right tile; some tile is full. `a_vals`: positive block entries.
All inputs are finite; a program needn't handle non-finite values. No bound on the sum of `keep` on one device may be relied on, other than what follows from the above.
Results may differ from a plain program's by a relative error of at most 0.0003.
Values may be sent and summed in bfloat16 or wider, within the bound.
A program may use at most 128 MiB of HBM per device.

v0:
```python
import jax
import jax.numpy as jnp
from jax import lax
from jax.sharding import PartitionSpec as P

ROWB = 2
KT = 32
COLB = 8


epsilon = 1e-06


def flatten_left(pieces):
    values, row_ids, col_ids, counts = pieces
    tile_side = values.shape[-1]
    many = values.shape[2]
    slots = values.shape[3]
    flat_vals = values.reshape(many * slots, tile_side, tile_side)
    owners = jnp.arange(many, dtype=jnp.int32)
    inner = (owners[:, None] * KT + col_ids.reshape(many, slots)).reshape(-1)
    live = (jnp.arange(slots, dtype=jnp.int32)[None, :] < counts.reshape(many)[:, None]).reshape(-1)
    return (flat_vals, inner, row_ids.reshape(-1), live)


def flatten_right(pieces, inner_tile):
    values, row_ids, col_ids, counts = pieces
    tile_side = values.shape[-1]
    many = values.shape[1]
    slots = values.shape[3]
    flat_vals = values.reshape(many * slots, tile_side, tile_side)
    owners = jnp.arange(many, dtype=jnp.int32)
    inner = (owners[:, None] * inner_tile + row_ids.reshape(many, slots)).reshape(-1)
    live = (jnp.arange(slots, dtype=jnp.int32)[None, :] < counts.reshape(many)[:, None]).reshape(-1)
    return (flat_vals, inner, col_ids.reshape(-1), live)


def left_term(left_set, right_set):
    left_vals, left_inner, left_rows, left_live = left_set
    right_vals, right_inner, right_cols, right_live = right_set
    tile_side = left_vals.shape[-1]
    match = left_live[:, None] & right_live[None, :] & (left_inner[:, None] == right_inner[None, :])
    placer = (
        match[:, :, None]
        & (right_cols[None, :, None] == jnp.arange(COLB, dtype=jnp.int32)[None, None, :])
    ).astype(jnp.bfloat16)
    right_rows = jnp.einsum(
        "stc,thw->shcw", placer, right_vals, preferred_element_type=jnp.bfloat16
    )
    right_rows = right_rows.reshape(left_vals.shape[0], tile_side, COLB * tile_side)
    terms = jnp.einsum("sha,sax->shx", left_vals, right_rows, preferred_element_type=jnp.float32)
    onehot = (left_rows[:, None] == jnp.arange(ROWB, dtype=jnp.int32)[None, :]).astype(jnp.float32)
    return jnp.einsum("sr,shx->rhx", onehot, terms, precision=lax.Precision.HIGHEST)


def shards(a_vals, a_rows, a_cols, a_count, b_vals, b_rows, b_cols, b_count, keep):
    tile_side = a_vals.shape[-1]
    rows_dev = keep.shape[0]
    row_devices = lax.axis_size("row")
    inner_tile = KT * lax.axis_size("col") // row_devices
    gathered_right = (
        lax.all_gather(b_vals, "row", axis=1, tiled=True),
        lax.all_gather(b_rows, "row", axis=1, tiled=True),
        lax.all_gather(b_cols, "row", axis=1, tiled=True),
        lax.all_gather(b_count, "row", axis=1, tiled=True),
    )
    right_set = flatten_right(gathered_right, inner_tile)
    partial_value = left_term(
        flatten_left(
            (
                lax.all_gather(a_vals, "col", axis=2, tiled=True),
                lax.all_gather(a_rows, "col", axis=2, tiled=True),
                lax.all_gather(a_cols, "col", axis=2, tiled=True),
                lax.all_gather(a_count, "col", axis=2, tiled=True),
            )
        ),
        right_set,
    )
    partial_value = partial_value.reshape(rows_dev * tile_side, COLB * tile_side)
    shared = lax.psum_scatter(partial_value, "depth", scatter_dimension=1, tiled=True)
    span_cols = shared.shape[1]
    pruned = jnp.where(keep[:, None, :] > 0, shared.reshape(rows_dev, tile_side, span_cols), 0.0)
    squares = pruned * pruned
    col_mass = lax.psum(jnp.sum(squares, axis=(0, 1)), "row") / (row_devices * rows_dev * tile_side)
    normed = squares / (col_mass + epsilon)
    return normed.reshape(rows_dev * tile_side, span_cols)


def solution(mesh):
    placed = (
        P("row", "depth", "col", None, None, None),
        P("row", "depth", "col", None),
        P("row", "depth", "col", None),
        P("row", "depth", "col"),
        P("depth", "row", "col", None, None, None),
        P("depth", "row", "col", None),
        P("depth", "row", "col", None),
        P("depth", "row", "col"),
        P("row", ("col", "depth")),
    )
    return jax.shard_map(
        shards, mesh=mesh, in_specs=placed, out_specs=P("row", ("col", "depth")), check_vma=False
    )
```

profile of v0, /device:TPU:2, one launch (start us, length us, event | category | flops | bytes accessed | tf_op | source)
XLA Modules:
  0.0 276.7 jit_solution(4198446448461696159)
XLA Ops:
  6.5 0.0 all-gather.3.cloned.1.call-start
  6.5 0.7 all-gather.3.cloned.1.call-update
  7.3 0.0 all-gather.5.cloned.1.call-start
  7.3 0.7 all-gather.5.cloned.1.call-update
  8.0 0.0 reduce-scatter.2.cloned.1.call-start
  8.7 1.3 dynamic-slice
  10.0 0.7 bitcast_dynamic-update-slice_fusion.1
  10.7 14.6 %all-reduce = s32[8]{0:T(128)S(1)} all-reduce(s32[8]{0:T(128)S(1)} %bitcast_dynamic-update-slice_fusion.1), channel_id=1, replica_groups=mesh['row'=16,'col'=8,'depth'=4] {'col'}, use_global_device_ids=true, to_apply=%add | all-reduce | flops 8 | bytes 64
  25.3 32.7 %all_gather.28 = s32[1,16,1,12]{3,2,0,1:T(1,128)S(1)} all-gather(s32[1,1,1,12]{3,2,0,1:T(1,128)} %bitcast.52), channel_id=1, replica_groups=mesh['row'=16,'col'=8,'depth'=4] {'row'}, dimensions={1}, use_global_device_ids=true | all-gather | bytes 816 | tf_op jit(solution)/shard_map/all_gather | solution.py:63
  58.0 0.5 broadcast.106
  58.5 0.7 reduce.14
  59.1 0.1 reshape.169
  59.2 0.1 add.41
  59.3 0.1 add.42
  59.4 20.5 %all_gather.27 = s32[1,1,8,4]{3,1,0,2:T(1,128)S(1)} all-gather(s32[1,1,1,4]{3,1,0,2:T(1,128)} %bitcast.53), channel_id=1, replica_groups=mesh['row'=16,'col'=8,'depth'=4] {'col'}, dimensions={2}, use_global_device_ids=true | all-gather | bytes 144 | tf_op jit(solution)/shard_map/all_gather | solution.py:73
  79.9 0.7 reduce.15
  80.6 0.1 reshape.168
  80.6 0.1 add.38
  80.7 0.1 add.39
  80.8 1.4 dynamic-slice.1
  82.8 0.7 bitcast_dynamic-update-slice_fusion
  83.5 18.6 %all-reduce.1 = s32[16]{0:T(128)S(1)} all-reduce(s32[16]{0:T(128)S(1)} %bitcast_dynamic-update-slice_fusion), channel_id=1, replica_groups=mesh['row'=16,'col'=8,'depth'=4] {'row'}, use_global_device_ids=true, to_apply=%add.1 | all-reduce | flops 16 | bytes 128
  102.2 0.1 iota_compare_fusion.1
  102.2 0.1 lt.53
  102.3 0.1 iota_compare_fusion.2
  102.4 0.1 lt.48
  102.5 27.1 %all_gather.29 = s32[1,16,1,12]{3,2,0,1:T(1,128)S(1)} all-gather(s32[1,1,1,12]{3,2,0,1:T(1,128)} %bitcast.54), channel_id=1, replica_groups=mesh['row'=16,'col'=8,'depth'=4] {'row'}, dimensions={1}, use_global_device_ids=true | all-gather | bytes 816 | tf_op jit(solution)/shard_map/all_gather | solution.py:64
  129.6 0.7 reduce.13
  130.2 0.1 eq.59
  130.3 18.5 %all_gather.24 = s32[1,1,8,4]{3,1,0,2:T(1,128)S(1)} all-gather(s32[1,1,1,4]{3,1,0,2:T(1,128)} %bitcast.55), channel_id=1, replica_groups=mesh['row'=16,'col'=8,'depth'=4] {'col'}, dimensions={2}, use_global_device_ids=true | all-gather | bytes 144 | tf_op jit(solution)/shard_map/all_gather | solution.py:72
  148.8 0.7 reduce.16
  149.5 0.1 eq.52
  149.6 0.1 compare_and_fusion
  149.7 0.0 all-gather.3.cloned.1.call-done
  149.7 10.8 %fusion.3 = bf16[32,128,8,128]{3,2,1,0:T(8,128)(2,1)} fusion(bf16[192,128,128]{2,1,0:T(8,128)(2,1)} %bitcast.47, pred[192,8]{0,1:T(8,128)(4,1)S(1)} %iota_compare_fusion, pred[32,192]{1,0:T(8,128)(4,1)S(1)} %compare_and_fusion), kind=kOutput, calls=%fused_computation.4 | convolution fusion | flops 1610661888 | bytes 14687744 | tf_op jit(solution)/shard_map/stc,thw->shcw/dot_general | solution.py:47
  160.5 12.4 %copy.26 = bf16[32,128,8,128]{1,3,2,0:T(8,128)(2,1)} copy(bf16[32,128,8,128]{3,2,1,0:T(8,128)(2,1)} %fusion.3) | data formatting | bytes 16777216 | tf_op jit(solution)/shard_map/reshape | solution.py:50
  173.0 0.0 all-gather.5.cloned.1.call-done
  173.0 11.7 %convolution_bitcast_fusion = f32[32,128,1024]{1,2,0:T(8,128)} fusion(bf16[32,128,1024]{1,2,0:T(8,128)(2,1)} %bitcast.46, bf16[32,128,128]{2,1,0:T(8,128)(2,1)} %bitcast.49), kind=kOutput, calls=%fused_computation | convolution fusion | flops 1073741824 | bytes 26214400 | tf_op jit(solution)/shard_map/sha,sax->shx/dot_general | solution.py:51
  184.6 16.6 %copy.22 = f32[32,128,1024]{2,0,1:T(8,128)} copy(f32[32,128,1024]{1,2,0:T(8,128)} %convolution_bitcast_fusion) | data formatting | bytes 33554432 | tf_op jit(solution)/shard_map/sha,sax->shx/dot_general | solution.py:51
  201.2 0.0 copy-start
  201.2 9.0 %fusion.12 = f32[2,128,1024]{2,0,1:T(2,128)S(1)} fusion(f32[32,128,1024]{2,0,1:T(8,128)} %copy.22, s32[32]{0:T(128)S(1)} %eq.52), kind=kOutput, calls=%fused_computation.16 | convolution fusion | flops 100663360 | bytes 17825920 | tf_op jit(solution)/shard_map/sr,shx->rhx/dot_general | solution.py:53
  210.3 1.3 copy.23
  211.6 0.0 reduce-scatter.2.cloned.1.call-update
  211.6 0.0 copy-done
  211.6 24.6 %reduce-scatter.2.cloned.1.call-done = f32[256,256]{1,0:T(8,128)} async-done(((f32[256,1024]{1,0:T(8,128)}), f32[256,256]{1,0:T(8,128)}) %reduce-scatter.2.cloned.1.call-update) | async-done | bytes 262160 | tf_op jit(solution)/shard_map/reduce_scatter | solution.py:80
  236.2 1.0 fusion.9
  237.2 31.3 %psum.7 = f32[256]{0:T(256)S(1)} all-reduce(f32[256]{0:T(256)S(1)} %fusion.9), channel_id=1, replica_groups=mesh['row'=16,'col'=8,'depth'=4] {'row'}, use_global_device_ids=true, to_apply=%region_2.3 | all-reduce | flops 256 | bytes 2048 | tf_op jit(solution)/shard_map/psum | solution.py:84
  268.5 1.7 fusion.8
  (9 shorter events, 0.0 us)
Async XLA Ops:
  6.5 143.2 %all-gather.3.cloned.1.call-start = ((), (), s32[]{:S(2)}) async-start(), calls=%async_computation.1 | async-start | bytes 6684672 | tf_op jit(solution)/shard_map/all_gather | solution.py:62
  7.3 165.7 %all-gather.5.cloned.1.call-start = ((), (), s32[]{:S(2)}) async-start(), calls=%async_computation.2 | async-start | bytes 1179648 | tf_op jit(solution)/shard_map/all_gather | solution.py:71
  8.0 228.2 %reduce-scatter.2.cloned.1.call-start = ((), (), s32[]{:S(2)}) async-start(), calls=%async_computation.3 | async-start | bytes 1310720 | tf_op jit(solution)/shard_map/reduce_scatter | solution.py:80
  201.2 10.4 %copy-start = (s32[2,256]{1,0:T(2,128)S(1)}, s32[2,256]{1,0:T(2,128)}, u32[]{:S(2)}) copy-start(s32[2,256]{1,0:T(2,128)} %param.17) | copy-start | bytes 6148
Sparse Core Ops, SparseCore 0:
  9.4 91.3 all-gather.2
  104.0 59.0 all-gather.4
  211.7 24.4 reduce-scatter.1
where the time goes:
time: 278 us; the launch traced here: 277 us
  blocking collectives  163 us (59%)
  local copies, waits for them, and re-layouts  35.7 us (13%)
  matrix products  31.5 us (11%)
  waiting for transfers between devices  26 us (9%)
  between operations  14.5 us (5%)
  other arithmetic  5.61 us (2%)
    unnamed x2, blocking collectives  33.2 us
    all_gather x1, blocking collectives, shards(): lax.all_gather(b_rows, 'row', axis=1, tiled=True)  32.7 us
    psum x1, blocking collectives, shards(): lax.psum(jnp.sum(squares, axis=(0, 1)), 'row')  31.3 us
    all_gather x1, blocking collectives, shards(): lax.all_gather(b_cols, 'row', axis=1, tiled=True)  27.1 us
    reduce_scatter x1, waiting for transfers between devices, shards(): lax.psum_scatter(partial_value, 'depth', scatter_dimension=1, tiled=True)  24.6 us
    all_gather x1, blocking collectives, shards(): lax.all_gather(a_cols, 'col', axis=2, tiled=True)  20.5 us
    all_gather x1, blocking collectives, shards(): lax.all_gather(a_rows, 'col', axis=2, tiled=True)  18.5 us
    dot_general x1, local copies, waits for them, and re-layouts, left_term(): jnp.einsum('sha,sax->shx', left_vals, right_rows, preferred_element_type=...  16.6 us
  transfers between devices with their start and end apart: 3, of which 1 were waited for; matrix products, arithmetic and copies ran while one was open for 11% of the time, Pallas kernels for 0%

commit v1 on v0

v1 whole, which is shorter than its diff:
```python
import jax
import jax.numpy as jnp
from jax import lax
from jax.experimental import pallas as pl
from jax.experimental.pallas import tpu as pltpu
from jax.sharding import PartitionSpec as P

BS = 128
ROWB = 2
KT = 32
COLB = 8
KBT = 16
NZA = 4
NZB = 12
N_ROW = 16
N_COL = 8
N_DEPTH = 4
HALF = NZB // 2
FAR = N_ROW // 2
ABSENT = NZB
LANES = 128
QUARTER = COLB * BS // N_DEPTH
ROWS = ROWB * BS
RIGHT, LEFT = 0, 1

epsilon = 1e-06
MESH = pl.DeviceIdType.MESH


def kernel(a_hbm, akey_ref, b_hbm, bkey_ref, keep_ref, sq_ref, mass_ref, *scratch):
    tiles = scratch[:N_ROW]
    (abuf, lhs, akeys, bkeys, table, table_s, acc, rs1, rs2, colsum, masses,
     local_sem, ring_send, ring_recv, a_send, a_recv, ak_send, ak_recv, bk_send, bk_recv,
     d1_send, d1_recv, d2_send, d2_recv, m_send, m_recv) = scratch[N_ROW:]
    row = lax.axis_index("row")
    col = lax.axis_index("col")
    depth = lax.axis_index("depth")
    y_lo, core = depth // 2, depth % 2
    sibling = y_lo * 2 + (1 - core)
    across = (1 - y_lo) * 2 + core
    across_sibling = (1 - y_lo) * 2 + (1 - core)

    def row_peer(k):
        return lax.rem(row + k, N_ROW)

    def col_peer(k):
        return lax.rem(col + k, N_COL)

    own_b = pltpu.make_async_copy(b_hbm, tiles[0].at[pl.ds(0, NZB)], local_sem.at[0])
    own_b.start()
    own_a = pltpu.make_async_copy(a_hbm, abuf.at[col], local_sem.at[1])
    own_a.start()

    barrier = pltpu.get_barrier_semaphore()
    for k in range(1, N_ROW):
        pl.semaphore_signal(barrier, inc=1, device_id={"row": row_peer(k)}, device_id_type=MESH)
    for k in range(1, N_COL):
        pl.semaphore_signal(barrier, inc=1, device_id={"col": col_peer(k)}, device_id_type=MESH)
    for other in (sibling, across):
        pl.semaphore_signal(barrier, inc=1, device_id={"depth": other}, device_id_type=MESH)
    pl.semaphore_wait(barrier, N_ROW - 1 + N_COL - 1 + 2)

    def tile_of(way, step):
        return tiles[step] if way == RIGHT or step == FAR else tiles[FAR + step]

    def hop(way, step, half):
        source = b_hbm if step == 1 else tile_of(way, step - 1)
        part = pl.ds(half * HALF, HALF)
        return pltpu.make_async_remote_copy(
            src_ref=source.at[part],
            dst_ref=tile_of(way, step).at[part],
            send_sem=ring_send.at[way, step, half],
            recv_sem=ring_recv.at[way, step, half],
            device_id={"row": row_peer(1 if way == RIGHT else N_ROW - 1)},
            device_id_type=MESH,
        )

    order = ((RIGHT, 0), (LEFT, 1), (RIGHT, 1), (LEFT, 0))

    def hops(step):
        return order if step < FAR else order[:2]

    def bkey_copy(k):
        return pltpu.make_async_remote_copy(
            src_ref=bkey_ref, dst_ref=bkeys.at[row], send_sem=bk_send.at[k], recv_sem=bk_recv.at[k],
            device_id={"row": row_peer(k)}, device_id_type=MESH)

    def akey_copy(k):
        return pltpu.make_async_remote_copy(
            src_ref=akey_ref, dst_ref=akeys.at[col], send_sem=ak_send.at[k], recv_sem=ak_recv.at[k],
            device_id={"col": col_peer(k)}, device_id_type=MESH)

    def a_copy(k):
        return pltpu.make_async_remote_copy(
            src_ref=a_hbm, dst_ref=abuf.at[col], send_sem=a_send.at[k], recv_sem=a_recv.at[k],
            device_id={"col": col_peer(k)}, device_id_type=MESH)

    for way, half in order:
        hop(way, 1, half).start()
    for k in range(1, N_ROW):
        bkey_copy(k).start()
    for k in range(1, N_COL):
        akey_copy(k).start()
    for k in range(1, N_COL):
        a_copy(k).start()

    bkeys[row] = bkey_ref[...]
    akeys[col] = akey_ref[...]
    for tile in tiles:
        tile[ABSENT] = jnp.zeros((BS, BS), jnp.bfloat16)
    acc[...] = jnp.zeros_like(acc)
    own_b.wait()
    own_a.wait()

    def prepare():
        for k in range(1, N_ROW):
            bkey_copy(k).wait_recv()
        for k in range(1, N_COL):
            akey_copy(k).wait_recv()
        lane = lax.broadcasted_iota(jnp.int32, (1, LANES), 1)
        for r in range(N_ROW):
            left = akeys[r // 2]
            wanted = left - (r % 2) * (KBT * COLB)
            have = bkeys[r]
            slot = jnp.full((1, LANES), ABSENT, jnp.int32)
            for t in range(NZB):
                slot = jnp.where(wanted == have[:, t:t + 1], t, slot)
            table[r] = jnp.where(lane < NZA * COLB, slot, left)
        move = pltpu.make_async_copy(table, table_s, local_sem.at[2])
        move.start()
        for k in range(1, N_COL):
            a_copy(k).wait_recv()
        move.wait()

        def stack(c, carry):
            for s in range(NZA):
                block = abuf[c, s]
                which = table_s[2 * c, 0, NZA * COLB + s]
                for i in range(ROWB):
                    lhs[c, i * BS:(i + 1) * BS, s * BS:(s + 1) * BS] = jnp.where(
                        which == i, block, jnp.zeros_like(block))
            return carry

        lax.fori_loop(0, N_COL, stack, 0)

    def multiply(index):
        tile = tiles[index]
        owner = lax.rem(row + (N_ROW - index if index <= FAR else index - FAR), N_ROW)
        left = lhs[owner // 2]

        def part(j, carry):
            strips = []
            for s in range(NZA):
                pair = [tile[table_s[owner, 0, s * COLB + 2 * j + e]] for e in range(2)]
                strips.append(jnp.concatenate(pair, axis=1))
            acc[j] += jnp.dot(left, jnp.concatenate(strips, axis=0), preferred_element_type=jnp.float32)
            return carry

        lax.fori_loop(0, N_DEPTH, part, 0)

    plan = {3: (0, 1, 9), 4: (2, 10, 3), 5: (11, 4, 12), 6: (5, 13), 7: (6, 14), 8: (7, 15)}
    for step in range(2, FAR + 1):
        ahead = hops(step)
        for way, half in order:
            hop(way, step - 1, half).wait_recv()
            if (way, half) in ahead:
                hop(way, step, half).start()
        if step == 3:
            prepare()
        for index in plan.get(step, ()):
            multiply(index)
    for way, half in hops(FAR):
        hop(way, FAR, half).wait_recv()
    multiply(FAR)

    def to_sibling(slot, half):
        part = pl.ds(half * BS, BS)
        which = across_sibling if slot == 0 else sibling
        return pltpu.make_async_remote_copy(
            src_ref=acc.at[which, part], dst_ref=rs1.at[slot, part],
            send_sem=d1_send.at[slot, half], recv_sem=d1_recv.at[slot, half],
            device_id={"depth": sibling}, device_id_type=MESH)

    def to_across(half):
        part = pl.ds(half * BS, BS)
        return pltpu.make_async_remote_copy(
            src_ref=acc.at[across, part], dst_ref=rs2.at[part],
            send_sem=d2_send.at[half], recv_sem=d2_recv.at[half],
            device_id={"depth": across}, device_id_type=MESH)

    for slot in range(2):
        for half in range(ROWB):
            to_sibling(slot, half).start()
    for half in range(ROWB):
        part = pl.ds(half * BS, BS)
        to_sibling(0, half).wait_recv()
        acc[across, part] += rs1[0, part]
        to_across(half).start()
    total = jnp.zeros((1, QUARTER), jnp.float32)
    for half in range(ROWB):
        part = pl.ds(half * BS, BS)
        to_sibling(1, half).wait_recv()
        mine = acc[depth, part] + rs1[1, part]
        to_across(half).wait_recv()
        product = mine + rs2[part]
        pruned = jnp.where(keep_ref[half:half + 1, :] > 0, product, 0.0)
        squares = pruned * pruned
        sq_ref[part] = squares
        total = total + jnp.sum(squares, axis=0, keepdims=True)
    colsum[...] = total
    masses[row] = total

    def mass_copy(k):
        return pltpu.make_async_remote_copy(
            src_ref=colsum, dst_ref=masses.at[row], send_sem=m_send.at[k], recv_sem=m_recv.at[k],
            device_id={"row": row_peer(k)}, device_id_type=MESH)

    for k in range(1, N_ROW):
        mass_copy(k).start()
    for k in range(1, N_ROW):
        mass_copy(k).wait_recv()
    mass_ref[...] = jnp.sum(masses[...], axis=0)

    for step in range(1, FAR + 1):
        for way, half in hops(step):
            hop(way, step, half).wait_send()
    for k in range(1, N_ROW):
        bkey_copy(k).wait_send()
        mass_copy(k).wait_send()
    for k in range(1, N_COL):
        akey_copy(k).wait_send()
        a_copy(k).wait_send()
    for half in range(ROWB):
        for slot in range(2):
            to_sibling(slot, half).wait_send()
        to_across(half).wait_send()


def shards(a_vals, a_rows, a_cols, a_count, b_vals, b_rows, b_cols, b_count, keep):
    rank = jnp.arange(COLB, dtype=jnp.int32)
    a_live = jnp.arange(NZA, dtype=jnp.int32) < a_count.reshape(())
    a_want = jnp.where(a_live[:, None], a_cols.reshape(NZA, 1) * COLB + rank[None, :], -5000)
    akey = jnp.concatenate([a_want.reshape(-1), a_rows.reshape(-1)])
    akey = jnp.pad(akey, (0, LANES - akey.shape[0]), constant_values=-5000).reshape(1, LANES)
    b_live = jnp.arange(NZB, dtype=jnp.int32) < b_count.reshape(())
    bkey = jnp.where(b_live, b_rows.reshape(NZB) * COLB + b_cols.reshape(NZB), -1000)
    bkey = jnp.pad(bkey, (0, LANES - NZB), constant_values=-1000).reshape(1, LANES)

    vmem = pl.BlockSpec(memory_space=pltpu.VMEM)
    hbm = pl.BlockSpec(memory_space=pl.ANY)
    dma = pltpu.SemaphoreType.DMA
    squares, mass = pl.pallas_call(
        kernel,
        out_shape=(
            jax.ShapeDtypeStruct((ROWS, QUARTER), jnp.float32),
            jax.ShapeDtypeStruct((1, QUARTER), jnp.float32),
        ),
        in_specs=[hbm, vmem, hbm, vmem, vmem],
        out_specs=(vmem, vmem),
        scratch_shapes=[pltpu.VMEM((NZB + 1, BS, BS), jnp.bfloat16)] * N_ROW
        + [
            pltpu.VMEM((N_COL, NZA, BS, BS), jnp.bfloat16),
            pltpu.VMEM((N_COL, ROWS, NZA * BS), jnp.bfloat16),
            pltpu.VMEM((N_COL, 1, LANES), jnp.int32),
            pltpu.VMEM((N_ROW, 1, LANES), jnp.int32),
            pltpu.VMEM((N_ROW, 1, LANES), jnp.int32),
            pltpu.SMEM((N_ROW, 1, LANES), jnp.int32),
            pltpu.VMEM((N_DEPTH, ROWS, QUARTER), jnp.float32),
            pltpu.VMEM((2, ROWS, QUARTER), jnp.float32),
            pltpu.VMEM((ROWS, QUARTER), jnp.float32),
            pltpu.VMEM((1, QUARTER), jnp.float32),
            pltpu.VMEM((N_ROW, 1, QUARTER), jnp.float32),
            dma((3,)),
            dma((2, FAR + 1, 2)),
            dma((2, FAR + 1, 2)),
            dma((N_COL,)),
            dma((N_COL,)),
            dma((N_COL,)),
            dma((N_COL,)),
            dma((N_ROW,)),
            dma((N_ROW,)),
            dma((2, ROWB)),
            dma((2, ROWB)),
            dma((ROWB,)),
            dma((ROWB,)),
            dma((N_ROW,)),
            dma((N_ROW,)),
        ],
        compiler_params=pltpu.CompilerParams(
            collective_id=0, has_side_effects=True, vmem_limit_bytes=40 << 20
        ),
    )(
        a_vals.reshape(NZA, BS, BS),
        akey,
        b_vals.reshape(NZB, BS, BS),
        bkey,
        keep,
    )
    return squares / (mass * (1.0 / (N_ROW * ROWS)) + epsilon)


def solution(mesh):
    placed = (
        P("row", "depth", "col", None, None, None),
        P("row", "depth", "col", None),
        P("row", "depth", "col", None),
        P("row", "depth", "col"),
        P("depth", "row", "col", None, None, None),
        P("depth", "row", "col", None),
        P("depth", "row", "col", None),
        P("depth", "row", "col"),
        P("row", ("col", "depth")),
    )
    return jax.shard_map(
        shards, mesh=mesh, in_specs=placed, out_specs=P("row", ("col", "depth")), check_vma=False
    )
```

time: 278 us -> 105 us (0.38)
  the two profiles are of different devices: /device:TPU:2 before, /device:TPU:1 now
where the time goes in v1:
time: 105 us
  Pallas kernels  98.5 us (94%)
  local copies, waits for them, and re-layouts  4.54 us (4%)
  between operations  1.34 us (1%)
    pallas_call x1, Pallas kernels, shards(): pl.pallas_call(kernel, out_shape=(jax.ShapeDtypeStruct((ROWS, QUARTER), j...  98.5 us
    unnamed x14, local copies, waits for them, and re-layouts  4.45 us

profile of v1, /device:TPU:1, one launch (start us, length us, event | category | flops | bytes accessed | tf_op | source)
XLA Modules:
  0.0 105.2 jit_solution(2788814797632640261)
XLA Ops:
  1.3 0.0 copy-start.3
  1.3 0.0 copy-start.4
  1.3 0.6 copy-done.3
  2.0 0.0 copy-done.4
  2.0 0.0 copy-start.5
  2.0 0.7 copy-done.5
  2.6 0.1 add_select_fusion
  2.7 0.0 copy-start.6
  2.7 0.1 select_n.13
  2.8 0.6 copy-done.6
  3.4 0.1 pad_add_fusion
  3.4 0.0 copy-start.2
  3.4 0.7 copy-done.2
  4.1 0.0 copy-start
  4.1 1.0 copy-done
  5.1 0.0 copy-start.1
  5.1 0.9 copy-done.1
  6.0 98.5 %shard_map.91 = (f32[256,256]{1,0:T(8,128)S(1)}, f32[1,256]{1,0:T(1,128)S(1)}) custom-call(bf16[4,128,128]{2,1,0:T(8,128)(2,1)S(1)} %bitcast.17, s32[1,128]{1,0:T(1,128)S(1)} %get-tuple-element.10.akey_ref, bf16[12,128,128]{2,1,0:T(8,128)(2,1)S(1)} %bitcast.16, s32[1,128]{1,0:T(1,128)S(1)} %get-tuple-element.9.bkey_ref, s32[2,256]{1,0:T(2,128)S(1)} %copy-done.2), custom_call_target="tpu_custom_call" | custom-call | tf_op jit(solution)/shard_map/pallas_call | solution.py:252
  104.5 0.7 broadcast_divide_fusion
  (5 shorter events, 0.0 us)
Async XLA Ops:
  1.3 0.7 copy-start.3
  1.3 0.7 copy-start.4
  2.0 0.7 copy-start.5
  2.7 0.7 copy-start.6
  3.4 0.7 copy-start.2
  4.1 1.0 copy-start
  5.1 0.9 copy-start.1

commit v2 on v1

--- a/solution.py
+++ b/solution.py
@@ -27,9 +27,11 @@
 MESH = pl.DeviceIdType.MESH
 
 
-def kernel(a_hbm, akey_ref, b_hbm, bkey_ref, keep_ref, sq_ref, mass_ref, *scratch):
+def kernel(a_hbm, arow_hbm, acol_hbm, acount_hbm, b_hbm, brow_hbm, bcol_hbm, bcount_hbm, keep_hbm,
+           flow_ref, *scratch):
     tiles = scratch[:N_ROW]
-    (abuf, lhs, akeys, bkeys, table, table_s, acc, rs1, rs2, colsum, masses,
+    (arow_s, acol_s, acount_s, brow_s, bcol_s, bcount_s, keep_ref, akey_ref, bkey_ref,
+     abuf, lhs, akeys, bkeys, table, table_s, acc, rs1, rs2, colsum, masses,
      local_sem, ring_send, ring_recv, a_send, a_recv, ak_send, ak_recv, bk_send, bk_recv,
      d1_send, d1_recv, d2_send, d2_recv, m_send, m_recv) = scratch[N_ROW:]
     row = lax.axis_index("row")
@@ -46,11 +48,6 @@
     def col_peer(k):
         return lax.rem(col + k, N_COL)
 
-    own_b = pltpu.make_async_copy(b_hbm, tiles[0].at[pl.ds(0, NZB)], local_sem.at[0])
-    own_b.start()
-    own_a = pltpu.make_async_copy(a_hbm, abuf.at[col], local_sem.at[1])
-    own_a.start()
-
     barrier = pltpu.get_barrier_semaphore()
     for k in range(1, N_ROW):
         pl.semaphore_signal(barrier, inc=1, device_id={"row": row_peer(k)}, device_id_type=MESH)
@@ -58,6 +55,35 @@
         pl.semaphore_signal(barrier, inc=1, device_id={"col": col_peer(k)}, device_id_type=MESH)
     for other in (sibling, across):
         pl.semaphore_signal(barrier, inc=1, device_id={"depth": other}, device_id_type=MESH)
+
+    own_b = pltpu.make_async_copy(b_hbm, tiles[0].at[pl.ds(0, NZB)], local_sem.at[0])
+    own_a = pltpu.make_async_copy(a_hbm, abuf.at[col], local_sem.at[1])
+    own_keep = pltpu.make_async_copy(keep_hbm, keep_ref, local_sem.at[3])
+    pairs = ((arow_hbm, arow_s), (acol_hbm, acol_s), (acount_hbm, acount_s),
+             (brow_hbm, brow_s), (bcol_hbm, bcol_s), (bcount_hbm, bcount_s))
+    small = [pltpu.make_async_copy(source, target, local_sem.at[4 + i])
+             for i, (source, target) in enumerate(pairs)]
+    for copy in small + [own_b, own_a, own_keep]:
+        copy.start()
+    for tile in tiles:
+        tile[ABSENT] = jnp.zeros((BS, BS), jnp.bfloat16)
+    acc[...] = jnp.zeros_like(acc)
+    for copy in small:
+        copy.wait()
+    lane = lax.broadcasted_iota(jnp.int32, (1, LANES), 1)
+    bkey = jnp.full((1, LANES), -1000, jnp.int32)
+    for t in range(NZB):
+        value = jnp.where(t < bcount_s[0, 0, 0], brow_s[t] * COLB + bcol_s[t], -1000)
+        bkey = jnp.where(lane == t, value, bkey)
+    akey = jnp.full((1, LANES), -5000, jnp.int32)
+    for s in range(NZA):
+        value = jnp.where(s < acount_s[0, 0, 0], acol_s[s] * COLB, -5000)
+        akey = jnp.where((lane >= s * COLB) & (lane < (s + 1) * COLB), value + lane - s * COLB, akey)
+        akey = jnp.where(lane == NZA * COLB + s, arow_s[s], akey)
+    akey_ref[...] = akey
+    bkey_ref[...] = bkey
+    akeys[col] = akey
+    bkeys[row] = bkey
     pl.semaphore_wait(barrier, N_ROW - 1 + N_COL - 1 + 2)
 
     def tile_of(way, step):
@@ -104,20 +130,15 @@
     for k in range(1, N_COL):
         a_copy(k).start()
 
-    bkeys[row] = bkey_ref[...]
-    akeys[col] = akey_ref[...]
-    for tile in tiles:
-        tile[ABSENT] = jnp.zeros((BS, BS), jnp.bfloat16)
-    acc[...] = jnp.zeros_like(acc)
     own_b.wait()
     own_a.wait()
+    own_keep.wait()
 
     def prepare():
         for k in range(1, N_ROW):
             bkey_copy(k).wait_recv()
         for k in range(1, N_COL):
             akey_copy(k).wait_recv()
-        lane = lax.broadcasted_iota(jnp.int32, (1, LANES), 1)
         for r in range(N_ROW):
             left = akeys[r // 2]
             wanted = left - (r % 2) * (KBT * COLB)
@@ -205,7 +226,7 @@
         product = mine + rs2[part]
         pruned = jnp.where(keep_ref[half:half + 1, :] > 0, product, 0.0)
         squares = pruned * pruned
-        sq_ref[part] = squares
+        flow_ref[part] = squares
         total = total + jnp.sum(squares, axis=0, keepdims=True)
     colsum[...] = total
     masses[row] = total
@@ -219,7 +240,8 @@
         mass_copy(k).start()
     for k in range(1, N_ROW):
         mass_copy(k).wait_recv()
-    mass_ref[...] = jnp.sum(masses[...], axis=0)
+    mass = jnp.sum(masses[...], axis=0) * (1.0 / (N_ROW * ROWS)) + epsilon
+    flow_ref[...] = flow_ref[...] / mass
 
     for step in range(1, FAR + 1):
         for way, half in hops(step):
@@ -237,28 +259,25 @@
 
 
 def shards(a_vals, a_rows, a_cols, a_count, b_vals, b_rows, b_cols, b_count, keep):
-    rank = jnp.arange(COLB, dtype=jnp.int32)
-    a_live = jnp.arange(NZA, dtype=jnp.int32) < a_count.reshape(())
-    a_want = jnp.where(a_live[:, None], a_cols.reshape(NZA, 1) * COLB + rank[None, :], -5000)
-    akey = jnp.concatenate([a_want.reshape(-1), a_rows.reshape(-1)])
-    akey = jnp.pad(akey, (0, LANES - akey.shape[0]), constant_values=-5000).reshape(1, LANES)
-    b_live = jnp.arange(NZB, dtype=jnp.int32) < b_count.reshape(())
-    bkey = jnp.where(b_live, b_rows.reshape(NZB) * COLB + b_cols.reshape(NZB), -1000)
-    bkey = jnp.pad(bkey, (0, LANES - NZB), constant_values=-1000).reshape(1, LANES)
-
     vmem = pl.BlockSpec(memory_space=pltpu.VMEM)
-    hbm = pl.BlockSpec(memory_space=pl.ANY)
+    hbm = pl.BlockSpec(memory_space=pltpu.HBM)
     dma = pltpu.SemaphoreType.DMA
-    squares, mass = pl.pallas_call(
+    return pl.pallas_call(
         kernel,
-        out_shape=(
-            jax.ShapeDtypeStruct((ROWS, QUARTER), jnp.float32),
-            jax.ShapeDtypeStruct((1, QUARTER), jnp.float32),
-        ),
-        in_specs=[hbm, vmem, hbm, vmem, vmem],
-        out_specs=(vmem, vmem),
+        out_shape=jax.ShapeDtypeStruct((ROWS, QUARTER), jnp.float32),
+        in_specs=[hbm] * 9,
+        out_specs=vmem,
         scratch_shapes=[pltpu.VMEM((NZB + 1, BS, BS), jnp.bfloat16)] * N_ROW
         + [
+            pltpu.SMEM((NZA,), jnp.int32),
+            pltpu.SMEM((NZA,), jnp.int32),
+            pltpu.SMEM((1, 1, 1), jnp.int32),
+            pltpu.SMEM((NZB,), jnp.int32),
+            pltpu.SMEM((NZB,), jnp.int32),
+            pltpu.SMEM((1, 1, 1), jnp.int32),
+            pltpu.VMEM((ROWB, QUARTER), jnp.int32),
+            pltpu.VMEM((1, LANES), jnp.int32),
+            pltpu.VMEM((1, LANES), jnp.int32),
             pltpu.VMEM((N_COL, NZA, BS, BS), jnp.bfloat16),
             pltpu.VMEM((N_COL, ROWS, NZA * BS), jnp.bfloat16),
             pltpu.VMEM((N_COL, 1, LANES), jnp.int32),
@@ -270,7 +289,7 @@
             pltpu.VMEM((ROWS, QUARTER), jnp.float32),
             pltpu.VMEM((1, QUARTER), jnp.float32),
             pltpu.VMEM((N_ROW, 1, QUARTER), jnp.float32),
-            dma((3,)),
+            dma((10,)),
             dma((2, FAR + 1, 2)),
             dma((2, FAR + 1, 2)),
             dma((N_COL,)),
@@ -287,16 +306,19 @@
             dma((N_ROW,)),
         ],
         compiler_params=pltpu.CompilerParams(
-            collective_id=0, has_side_effects=True, vmem_limit_bytes=40 << 20
+            collective_id=0, has_side_effects=True, vmem_limit_bytes=64 << 20
         ),
     )(
         a_vals.reshape(NZA, BS, BS),
-        akey,
+        a_rows.reshape(NZA),
+        a_cols.reshape(NZA),
+        a_count,
         b_vals.reshape(NZB, BS, BS),
-        bkey,
+        b_rows.reshape(NZB),
+        b_cols.reshape(NZB),
+        b_count,
         keep,
     )
-    return squares / (mass * (1.0 / (N_ROW * ROWS)) + epsilon)
 
 
 def solution(mesh):

time: 105 us -> 102 us (0.971)
  local copies, waits for them, and re-layouts: 4.54 us -> 1.67 us
    unnamed x14 -> x1, local copies, waits for them, and re-layouts: 4.45 us -> 1.67 us
where the time goes in v2:
time: 102 us
  Pallas kernels  99.1 us (97%)
  local copies, waits for them, and re-layouts  1.67 us (2%)
  between operations  1.3 us (1%)
    pallas_call x1, Pallas kernels, shards(): pl.pallas_call(kernel, out_shape=jax.ShapeDtypeStruct((ROWS, QUARTER), jn...  99.1 us

profile of v2, /device:TPU:1, one launch (start us, length us, event | category | flops | bytes accessed | tf_op | source)
XLA Modules:
  0.0 102.1 jit_solution(15935162162031691218)
XLA Ops:
  1.3 99.1 %shard_map.91 = f32[256,256]{1,0:T(8,128)} custom-call(bf16[4,128,128]{2,1,0:T(8,128)(2,1)} %bitcast.7, s32[4]{0:T(128)} %bitcast.8, s32[4]{0:T(128)} %bitcast.9, s32[1,1,1]{2,1,0:T(1,128)S(6)} %copy.11.acount_hbm, bf16[12,128,128]{2,1,0:T(8,128)(2,1)} %bitcast.6, s32[12]{0:T(128)} %bitcast.10, s32[12]{0:T(128)} %bitcast.11, ...), custom_call_target="tpu_custom_call" | custom-call | tf_op jit(solution)/shard_map/pallas_call | solution.py:265
  100.4 1.7 %copy.13 = f32[256,256]{1,0:T(8,128)} copy(f32[256,256]{1,0:T(8,128)} %shard_map.91) | data formatting | bytes 524288

commit v3 on v2

--- a/solution.py
+++ b/solution.py
@@ -22,12 +22,21 @@
 QUARTER = COLB * BS // N_DEPTH
 ROWS = ROWB * BS
 RIGHT, LEFT = 0, 1
+PITCH = 16
+IDS = N_ROW * PITCH
+PER_ROUND = 1
+ROUNDS = 26
+LAG = 3
+OWN = 1
+NEAR = OWN + NZB
+FRESH = NEAR + 2 * NZB
+HELD = FRESH + 2 * ROUNDS * PER_ROUND
 
 epsilon = 1e-06
 MESH = pl.DeviceIdType.MESH
 
 
-def kernel(a_hbm, arow_hbm, acol_hbm, acount_hbm, b_hbm, brow_hbm, bcol_hbm, bcount_hbm, keep_hbm,
+def full_ring(a_hbm, arow_hbm, acol_hbm, acount_hbm, b_hbm, brow_hbm, bcol_hbm, bcount_hbm, keep_hbm,
            flow_ref, *scratch):
     tiles = scratch[:N_ROW]
     (arow_s, acol_s, acount_s, brow_s, bcol_s, bcount_s, keep_ref, akey_ref, bkey_ref,
@@ -258,57 +267,362 @@
         to_across(half).wait_send()
 
 
+def sparse_ring(a_hbm, arow_hbm, acol_hbm, acount_hbm, b_hbm, brow_hbm, bcol_hbm, bcount_hbm, keep_hbm,
+                flow_ref, over_ref, *scratch):
+    (arow_s, acol_s, acount_s, brow_s, bcol_s, bcount_s, keep_ref, a_note, b_note, need_note,
+     abuf, lhs, a_notes, b_notes, needs, table, table_s, plan, plan_s, places, places_s,
+     store, stage, landing, flag_note, flags, depth_note, depth_flags,
+     acc, rs1, rs2, colsum, masses,
+     local_sem, hop_send, hop_recv, round_send, round_recv, a_send, a_recv, an_send, an_recv,
+     bn_send, bn_recv, n_send, n_recv, f_send, f_recv, g_send, g_recv,
+     d1_send, d1_recv, d2_send, d2_recv, m_send, m_recv) = scratch
+    row = lax.axis_index("row")
+    col = lax.axis_index("col")
+    depth = lax.axis_index("depth")
+    y_lo, core = depth // 2, depth % 2
+    sibling = y_lo * 2 + (1 - core)
+    across = (1 - y_lo) * 2 + core
+    across_sibling = (1 - y_lo) * 2 + (1 - core)
+
+    def row_peer(k):
+        return lax.rem(row + k, N_ROW)
+
+    def col_peer(k):
+        return lax.rem(col + k, N_COL)
+
+    def depth_peer(k):
+        return lax.rem(depth + k, N_DEPTH)
+
+    barrier = pltpu.get_barrier_semaphore()
+    for k in range(1, N_ROW):
+        pl.semaphore_signal(barrier, inc=1, device_id={"row": row_peer(k)}, device_id_type=MESH)
+    for k in range(1, N_COL):
+        pl.semaphore_signal(barrier, inc=1, device_id={"col": col_peer(k)}, device_id_type=MESH)
+    for k in range(1, N_DEPTH):
+        pl.semaphore_signal(barrier, inc=1, device_id={"depth": depth_peer(k)}, device_id_type=MESH)
+
+    own_b = pltpu.make_async_copy(b_hbm, store.at[pl.ds(OWN, NZB)], local_sem.at[0])
+    own_a = pltpu.make_async_copy(a_hbm, abuf.at[col], local_sem.at[1])
+    own_keep = pltpu.make_async_copy(keep_hbm, keep_ref, local_sem.at[3])
+    pairs = ((arow_hbm, arow_s), (acol_hbm, acol_s), (acount_hbm, acount_s),
+             (brow_hbm, brow_s), (bcol_hbm, bcol_s), (bcount_hbm, bcount_s))
+    small = [pltpu.make_async_copy(source, target, local_sem.at[4 + i])
+             for i, (source, target) in enumerate(pairs)]
+    for copy in small + [own_b, own_a, own_keep]:
+        copy.start()
+    store[0] = jnp.zeros((BS, BS), jnp.bfloat16)
+    acc[...] = jnp.zeros_like(acc)
+    for copy in small:
+        copy.wait()
+    wide = lax.broadcasted_iota(jnp.int32, (1, IDS), 1)
+    b_line = jnp.full((1, IDS), -1000, jnp.int32)
+    for t in range(NZB):
+        value = jnp.where(t < bcount_s[0, 0, 0], brow_s[t] * COLB + bcol_s[t], -1000)
+        b_line = jnp.where(wide == row * PITCH + t, value, b_line)
+    b_note[...] = b_line
+    b_notes[row] = b_line
+    here = wide // (2 * PITCH) == col
+    odd = (wide // PITCH) % 2
+    a_line = jnp.full((1, IDS), -5000, jnp.int32)
+    for s in range(NZA):
+        value = jnp.where(s < acount_s[0, 0, 0], acol_s[s] * COLB, -5000)
+        a_line = jnp.where((wide >= s * COLB) & (wide < (s + 1) * COLB), value + wide - s * COLB, a_line)
+        a_line = jnp.where(wide == NZA * COLB + s, arow_s[s], a_line)
+        a_note[s:s + 1, :] = jnp.where(here, value - odd * (KBT * COLB), -5000)
+    a_note[NZA:, :] = jnp.broadcast_to(a_line, (8 - NZA, IDS))
+    a_notes[col] = a_note[...]
+    pl.semaphore_wait(barrier, N_ROW - 1 + N_COL - 1 + N_DEPTH - 1)
+
+    def toward(way):
+        return {"row": row_peer(1 if way == RIGHT else N_ROW - 1)}
+
+    def hop(way):
+        return pltpu.make_async_remote_copy(
+            src_ref=b_hbm, dst_ref=store.at[pl.ds(NEAR + way * NZB, NZB)],
+            send_sem=hop_send.at[way], recv_sem=hop_recv.at[way],
+            device_id=toward(way), device_id_type=MESH)
+
+    def round_copy(way, k):
+        return pltpu.make_async_remote_copy(
+            src_ref=stage.at[way, k], dst_ref=landing.at[way, k],
+            send_sem=round_send.at[way, k], recv_sem=round_recv.at[way, k],
+            device_id=toward(way), device_id_type=MESH)
+
+    def b_note_copy(k):
+        return pltpu.make_async_remote_copy(
+            src_ref=b_note, dst_ref=b_notes.at[row], send_sem=bn_send.at[k], recv_sem=bn_recv.at[k],
+            device_id={"row": row_peer(k)}, device_id_type=MESH)
+
+    def need_copy(k):
+        return pltpu.make_async_remote_copy(
+            src_ref=need_note, dst_ref=needs.at[row], send_sem=n_send.at[k], recv_sem=n_recv.at[k],
+            device_id={"row": row_peer(k)}, device_id_type=MESH)
+
+    def a_note_copy(k):
+        return pltpu.make_async_remote_copy(
+            src_ref=a_note, dst_ref=a_notes.at[col], send_sem=an_send.at[k], recv_sem=an_recv.at[k],
+            device_id={"col": col_peer(k)}, device_id_type=MESH)
+
+    def a_copy(k):
+        return pltpu.make_async_remote_copy(
+            src_ref=a_hbm, dst_ref=abuf.at[col], send_sem=a_send.at[k], recv_sem=a_recv.at[k],
+            device_id={"col": col_peer(k)}, device_id_type=MESH)
+
+    def flag_copy(k):
+        return pltpu.make_async_remote_copy(
+            src_ref=flag_note, dst_ref=flags.at[col], send_sem=f_send.at[k], recv_sem=f_recv.at[k],
+            device_id={"col": col_peer(k)}, device_id_type=MESH)
+
+    def depth_flag_copy(k):
+        return pltpu.make_async_remote_copy(
+            src_ref=depth_note, dst_ref=depth_flags.at[depth], send_sem=g_send.at[k], recv_sem=g_recv.at[k],
+            device_id={"depth": depth_peer(k)}, device_id_type=MESH)
+
+    for k in range(1, N_COL):
+        a_note_copy(k).start()
+    for k in range(1, N_ROW):
+        b_note_copy(k).start()
+
+    for k in range(1, N_ROW):
+        b_note_copy(k).wait_recv()
+    for k in range(1, N_COL):
+        a_note_copy(k).wait_recv()
+    blocks = b_notes[0]
+    for r in range(1, N_ROW):
+        blocks = jnp.maximum(blocks, b_notes[r])
+    wants = a_notes[0]
+    for c in range(1, N_COL):
+        wants = jnp.maximum(wants, a_notes[c])
+    gap = blocks - wants[:NZA, :]
+    hit = jnp.where((gap >= 0) & (gap < COLB), 1, 0)
+    need = jnp.max(hit, axis=0, keepdims=True)
+    need_note[...] = need
+    needs[row] = need
+    for k in range(1, N_ROW):
+        need_copy(k).start()
+    for way in (RIGHT, LEFT):
+        hop(way).start()
+    for k in range(1, N_COL):
+        a_copy(k).start()
+
+    lane = lax.broadcasted_iota(jnp.int32, (1, LANES), 1)
+    for c in range(N_COL):
+        left = a_notes[c][NZA:NZA + 1, :LANES]
+        slot = jnp.full((1, LANES), PITCH - 1, jnp.int32)
+        for h in range(2):
+            for t in range(NZB):
+                at = (2 * c + h) * PITCH + t
+                slot = jnp.where(left == blocks[:, at:at + 1] + h * (KBT * COLB), at, slot)
+        table[c] = jnp.where(lane < NZA * COLB, slot, left)
+    move = pltpu.make_async_copy(table, table_s, local_sem.at[2])
+    move.start()
+
+    z = lax.broadcasted_iota(jnp.int32, (N_ROW, IDS), 0)
+    ident = lax.broadcasted_iota(jnp.int32, (N_ROW, IDS), 1)
+    origin, spot = ident // PITCH, ident % PITCH
+    apart = ((z - origin + N_ROW) % N_ROW, (origin - z + N_ROW) % N_ROW)
+    reach = (jnp.where(spot < HALF, FAR, FAR - 1), jnp.where(spot < HALF, FAR - 1, FAR))
+    for k in range(1, N_ROW):
+        need_copy(k).wait_recv()
+    wanted = jnp.concatenate([needs[r] for r in range(N_ROW)], axis=0)
+    left_to_go, where_at = [], []
+    for way in (RIGHT, LEFT):
+        inside = (wanted > 0) & (apart[way] >= 1) & (apart[way] <= reach[way])
+        last = jnp.max(jnp.where(inside, apart[way], 0), axis=0, keepdims=True)
+        left_to_go.append(jnp.where(apart[way] == 1, jnp.maximum(last - 1, 0), 0))
+        where_at.append(jnp.where((apart[way] == 1) & (spot < NZB), NEAR + way * NZB + spot, 0))
+    slot_of = lax.broadcasted_iota(jnp.int32, (N_ROW, LANES), 1)
+    zero_plan = jnp.zeros((N_ROW, LANES), jnp.int32)
+
+    waiting = [jnp.minimum(togo, 0) for togo in left_to_go for _ in range(LAG - 1)]
+
+    def one_round(k, state):
+        state = list(state)
+        for way in (RIGHT, LEFT):
+            togo, at, chosen = state[way], state[2 + way], state[4 + way]
+            queue = state[6 + way * (LAG - 1):6 + (way + 1) * (LAG - 1)]
+            moved = jnp.zeros_like(togo)
+            landed = jnp.zeros_like(togo)
+            for m in range(PER_ROUND):
+                rank = jnp.where(togo > 0, togo * IDS + ident, 0)
+                best = jnp.max(rank, axis=1, keepdims=True)
+                pick = (rank == best) & (togo > 0)
+                source = jnp.max(jnp.where(pick, at, 0), axis=1, keepdims=True)
+                number = k * PER_ROUND + m
+                chosen = jnp.where(slot_of == number, source, chosen)
+                moved = jnp.where(pick, togo - 1, moved)
+                landed = jnp.where(pick, FRESH + way * ROUNDS * PER_ROUND + number, landed)
+                togo = jnp.where(pick, 0, togo)
+            turn = 1 if way == RIGHT else N_ROW - 1
+            queue = [pltpu.roll(moved, turn, 0), *queue]
+            state[way] = togo + queue.pop()
+            state[6 + way * (LAG - 1):6 + (way + 1) * (LAG - 1)] = queue
+            state[2 + way] = jnp.maximum(at, pltpu.roll(landed, turn, 0))
+            state[4 + way] = chosen
+        return tuple(state)
+
+    state = lax.fori_loop(0, ROUNDS, one_round, (*left_to_go, *where_at, zero_plan, zero_plan, *waiting))
+    plan[RIGHT] = state[4]
+    plan[LEFT] = state[5]
+    plan_move = pltpu.make_async_copy(plan, plan_s, local_sem.at[10])
+    plan_move.start()
+    own_at = jnp.where((apart[0] == 0) & (spot < NZB), OWN + spot, 0)
+    final = jnp.maximum(jnp.maximum(state[2], state[3]), own_at)
+    places[0] = final[:, :LANES]
+    places[1] = final[:, LANES:]
+    places_move = pltpu.make_async_copy(places, places_s, local_sem.at[11])
+    places_move.start()
+    undone = jnp.maximum(state[0], state[1])
+    for late in state[6:]:
+        undone = jnp.maximum(undone, late)
+    undone = jnp.max(undone, axis=0, keepdims=True)
+    undone = jnp.maximum(undone[:, :LANES], undone[:, LANES:])
+    flag_note[...] = undone
+    flags[col] = undone
+    own_b.wait()
+    own_a.wait()
+    own_keep.wait()
+    for way in (RIGHT, LEFT):
+        hop(way).wait_recv()
+    plan_move.wait()
+
+    def middle(k):
+        if k == 0:
+            for i in range(1, N_COL):
+                flag_copy(i).start()
+        if k == 8:
+            move.wait()
+            for i in range(1, N_COL):
+                a_copy(i).wait_recv()
+
+        if 8 <= k < 8 + N_COL:
+            for c in (k - 8,):
+                for s in range(NZA):
+                    block = abuf[c, s]
+                    which = table_s[c, 0, NZA * COLB + s]
+                    for i in range(ROWB):
+                        lhs[c, i * BS:(i + 1) * BS, s * BS:(s + 1) * BS] = jnp.where(
+                            which == i, block, jnp.zeros_like(block))
+        if k == 18:
+            for i in range(1, N_COL):
+                flag_copy(i).wait_recv()
+            total = flags[0]
+            for c in range(1, N_COL):
+                total = jnp.maximum(total, flags[c])
+            depth_note[...] = total
+            depth_flags[depth] = total
+            for i in range(1, N_DEPTH):
+                depth_flag_copy(i).start()
+
+    for k in range(ROUNDS + LAG):
+        for way in (RIGHT, LEFT):
+            if k >= LAG:
+                round_copy(way, k - LAG).wait_recv()
+                for m in range(PER_ROUND):
+                    at = FRESH + (way * ROUNDS + k - LAG) * PER_ROUND + m
+                    store[at] = landing[way, k - LAG, m]
+            if k < ROUNDS:
+                for m in range(PER_ROUND):
+                    stage[way, k, m] = store[plan_s[way, row, k * PER_ROUND + m]]
+                round_copy(way, k).start()
+        middle(k)
+    places_move.wait()
+
+    def part(j, carry):
+        for c in range(N_COL):
+            strips = []
+            for s in range(NZA):
+                pair = []
+                for e in range(2):
+                    at = table_s[c, 0, s * COLB + 2 * j + e]
+                    pair.append(store[places_s[at // LANES, row, at % LANES]])
+                strips.append(jnp.concatenate(pair, axis=1))
+            acc[j] += jnp.dot(lhs[c], jnp.concatenate(strips, axis=0), preferred_element_type=jnp.float32)
+        return carry
+
+    lax.fori_loop(0, N_DEPTH, part, 0)
+
+    def to_sibling(slot, half):
+        part = pl.ds(half * BS, BS)
+        which = across_sibling if slot == 0 else sibling
+        return pltpu.make_async_remote_copy(
+            src_ref=acc.at[which, part], dst_ref=rs1.at[slot, part],
+            send_sem=d1_send.at[slot, half], recv_sem=d1_recv.at[slot, half],
+            device_id={"depth": sibling}, device_id_type=MESH)
+
+    def to_across(half):
+        part = pl.ds(half * BS, BS)
+        return pltpu.make_async_remote_copy(
+            src_ref=acc.at[across, part], dst_ref=rs2.at[part],
+            send_sem=d2_send.at[half], recv_sem=d2_recv.at[half],
+            device_id={"depth": across}, device_id_type=MESH)
+
+    for slot in range(2):
+        for half in range(ROWB):
+            to_sibling(slot, half).start()
+    for half in range(ROWB):
+        part = pl.ds(half * BS, BS)
+        to_sibling(0, half).wait_recv()
+        acc[across, part] += rs1[0, part]
+        to_across(half).start()
+    total = jnp.zeros((1, QUARTER), jnp.float32)
+    for half in range(ROWB):
+        part = pl.ds(half * BS, BS)
+        to_sibling(1, half).wait_recv()
+        mine = acc[depth, part] + rs1[1, part]
+        to_across(half).wait_recv()
+        product = mine + rs2[part]
+        pruned = jnp.where(keep_ref[half:half + 1, :] > 0, product, 0.0)
+        squares = pruned * pruned
+        flow_ref[part] = squares
+        total = total + jnp.sum(squares, axis=0, keepdims=True)
+    colsum[...] = total
+    masses[row] = total
+
+    def mass_copy(k):
+        return pltpu.make_async_remote_copy(
+            src_ref=colsum, dst_ref=masses.at[row], send_sem=m_send.at[k], recv_sem=m_recv.at[k],
+            device_id={"row": row_peer(k)}, device_id_type=MESH)
+
+    for k in range(1, N_ROW):
+        mass_copy(k).start()
+    for k in range(1, N_ROW):
+        mass_copy(k).wait_recv()
+    mass = jnp.sum(masses[...], axis=0) * (1.0 / (N_ROW * ROWS)) + epsilon
+    flow_ref[...] = flow_ref[...] / mass
+
+    for i in range(1, N_DEPTH):
+        depth_flag_copy(i).wait_recv()
+    over = depth_flags[0]
+    for i in range(1, N_DEPTH):
+        over = jnp.maximum(over, depth_flags[i])
+    over_ref[...] = jnp.broadcast_to(jnp.max(over, axis=1, keepdims=True), (1, LANES))
+
+    for way in (RIGHT, LEFT):
+        hop(way).wait_send()
+        for k in range(ROUNDS):
+            round_copy(way, k).wait_send()
+    for k in range(1, N_ROW):
+        b_note_copy(k).wait_send()
+        need_copy(k).wait_send()
+        mass_copy(k).wait_send()
+    for k in range(1, N_COL):
+        a_note_copy(k).wait_send()
+        a_copy(k).wait_send()
+        flag_copy(k).wait_send()
+    for k in range(1, N_DEPTH):
+        depth_flag_copy(k).wait_send()
+    for half in range(ROWB):
+        for slot in range(2):
+            to_sibling(slot, half).wait_send()
+        to_across(half).wait_send()
+
+
 def shards(a_vals, a_rows, a_cols, a_count, b_vals, b_rows, b_cols, b_count, keep):
     vmem = pl.BlockSpec(memory_space=pltpu.VMEM)
     hbm = pl.BlockSpec(memory_space=pltpu.HBM)
     dma = pltpu.SemaphoreType.DMA
-    return pl.pallas_call(
-        kernel,
-        out_shape=jax.ShapeDtypeStruct((ROWS, QUARTER), jnp.float32),
-        in_specs=[hbm] * 9,
-        out_specs=vmem,
-        scratch_shapes=[pltpu.VMEM((NZB + 1, BS, BS), jnp.bfloat16)] * N_ROW
-        + [
-            pltpu.SMEM((NZA,), jnp.int32),
-            pltpu.SMEM((NZA,), jnp.int32),
-            pltpu.SMEM((1, 1, 1), jnp.int32),
-            pltpu.SMEM((NZB,), jnp.int32),
-            pltpu.SMEM((NZB,), jnp.int32),
-            pltpu.SMEM((1, 1, 1), jnp.int32),
-            pltpu.VMEM((ROWB, QUARTER), jnp.int32),
-            pltpu.VMEM((1, LANES), jnp.int32),
-            pltpu.VMEM((1, LANES), jnp.int32),
-            pltpu.VMEM((N_COL, NZA, BS, BS), jnp.bfloat16),
-            pltpu.VMEM((N_COL, ROWS, NZA * BS), jnp.bfloat16),
-            pltpu.VMEM((N_COL, 1, LANES), jnp.int32),
-            pltpu.VMEM((N_ROW, 1, LANES), jnp.int32),
-            pltpu.VMEM((N_ROW, 1, LANES), jnp.int32),
-            pltpu.SMEM((N_ROW, 1, LANES), jnp.int32),
-            pltpu.VMEM((N_DEPTH, ROWS, QUARTER), jnp.float32),
-            pltpu.VMEM((2, ROWS, QUARTER), jnp.float32),
-            pltpu.VMEM((ROWS, QUARTER), jnp.float32),
-            pltpu.VMEM((1, QUARTER), jnp.float32),
-            pltpu.VMEM((N_ROW, 1, QUARTER), jnp.float32),
-            dma((10,)),
-            dma((2, FAR + 1, 2)),
-            dma((2, FAR + 1, 2)),
-            dma((N_COL,)),
-            dma((N_COL,)),
-            dma((N_COL,)),
-            dma((N_COL,)),
-            dma((N_ROW,)),
-            dma((N_ROW,)),
-            dma((2, ROWB)),
-            dma((2, ROWB)),
-            dma((ROWB,)),
-            dma((ROWB,)),
-            dma((N_ROW,)),
-            dma((N_ROW,)),
-        ],
-        compiler_params=pltpu.CompilerParams(
-            collective_id=0, has_side_effects=True, vmem_limit_bytes=64 << 20
-        ),
-    )(
+    inputs = (
         a_vals.reshape(NZA, BS, BS),
         a_rows.reshape(NZA),
         a_cols.reshape(NZA),
@@ -319,6 +633,100 @@
         b_count,
         keep,
     )
+    flow = jax.ShapeDtypeStruct((ROWS, QUARTER), jnp.float32)
+    words = [
+        pltpu.SMEM((NZA,), jnp.int32),
+        pltpu.SMEM((NZA,), jnp.int32),
+        pltpu.SMEM((1, 1, 1), jnp.int32),
+        pltpu.SMEM((NZB,), jnp.int32),
+        pltpu.SMEM((NZB,), jnp.int32),
+        pltpu.SMEM((1, 1, 1), jnp.int32),
+        pltpu.VMEM((ROWB, QUARTER), jnp.int32),
+    ]
+    sums = [
+        pltpu.VMEM((N_DEPTH, ROWS, QUARTER), jnp.float32),
+        pltpu.VMEM((2, ROWS, QUARTER), jnp.float32),
+        pltpu.VMEM((ROWS, QUARTER), jnp.float32),
+        pltpu.VMEM((1, QUARTER), jnp.float32),
+        pltpu.VMEM((N_ROW, 1, QUARTER), jnp.float32),
+    ]
+    tail = [dma((2, ROWB))] * 2 + [dma((ROWB,))] * 2 + [dma((N_ROW,))] * 2
+    left = [
+        pltpu.VMEM((N_COL, NZA, BS, BS), jnp.bfloat16),
+        pltpu.VMEM((N_COL, ROWS, NZA * BS), jnp.bfloat16),
+    ]
+
+    def full():
+        return pl.pallas_call(
+            full_ring,
+            out_shape=flow,
+            in_specs=[hbm] * 9,
+            out_specs=vmem,
+            scratch_shapes=[pltpu.VMEM((NZB + 1, BS, BS), jnp.bfloat16)] * N_ROW
+            + words
+            + [pltpu.VMEM((1, LANES), jnp.int32)] * 2
+            + left
+            + [
+                pltpu.VMEM((N_COL, 1, LANES), jnp.int32),
+                pltpu.VMEM((N_ROW, 1, LANES), jnp.int32),
+                pltpu.VMEM((N_ROW, 1, LANES), jnp.int32),
+                pltpu.SMEM((N_ROW, 1, LANES), jnp.int32),
+            ]
+            + sums
+            + [dma((10,))]
+            + [dma((2, FAR + 1, 2))] * 2
+            + [dma((N_COL,))] * 4
+            + [dma((N_ROW,))] * 2
+            + tail,
+            compiler_params=pltpu.CompilerParams(
+                collective_id=1, has_side_effects=True, vmem_limit_bytes=64 << 20
+            ),
+        )(*inputs)
+
+    result, over = pl.pallas_call(
+        sparse_ring,
+        out_shape=(flow, jax.ShapeDtypeStruct((1, LANES), jnp.int32)),
+        in_specs=[hbm] * 9,
+        out_specs=(vmem, vmem),
+        scratch_shapes=words
+        + [
+            pltpu.VMEM((8, IDS), jnp.int32),
+            pltpu.VMEM((1, IDS), jnp.int32),
+            pltpu.VMEM((1, IDS), jnp.int32),
+        ]
+        + left
+        + [
+            pltpu.VMEM((N_COL, 8, IDS), jnp.int32),
+            pltpu.VMEM((N_ROW, 1, IDS), jnp.int32),
+            pltpu.VMEM((N_ROW, 1, IDS), jnp.int32),
+            pltpu.VMEM((N_COL, 1, LANES), jnp.int32),
+            pltpu.SMEM((N_COL, 1, LANES), jnp.int32),
+            pltpu.VMEM((2, N_ROW, LANES), jnp.int32),
+            pltpu.SMEM((2, N_ROW, LANES), jnp.int32),
+            pltpu.VMEM((2, N_ROW, LANES), jnp.int32),
+            pltpu.SMEM((2, N_ROW, LANES), jnp.int32),
+            pltpu.VMEM((HELD, BS, BS), jnp.bfloat16),
+            pltpu.VMEM((2, ROUNDS, PER_ROUND, BS, BS), jnp.bfloat16),
+            pltpu.VMEM((2, ROUNDS, PER_ROUND, BS, BS), jnp.bfloat16),
+            pltpu.VMEM((1, LANES), jnp.int32),
+            pltpu.VMEM((N_COL, 1, LANES), jnp.int32),
+            pltpu.VMEM((1, LANES), jnp.int32),
+            pltpu.VMEM((N_DEPTH, 1, LANES), jnp.int32),
+        ]
+        + sums
+        + [dma((12,))]
+        + [dma((2,))] * 2
+        + [dma((2, ROUNDS))] * 2
+        + [dma((N_COL,))] * 4
+        + [dma((N_ROW,))] * 4
+        + [dma((N_COL,))] * 2
+        + [dma((N_DEPTH,))] * 2
+        + tail,
+        compiler_params=pltpu.CompilerParams(
+            collective_id=0, has_side_effects=True, vmem_limit_bytes=64 << 20
+        ),
+    )(*inputs)
+    return lax.cond(over[0, 0] > 0, full, lambda: result)
 
 
 def solution(mesh):

time: 102 us -> 94.5 us (0.926)
  Pallas kernels: 99.1 us -> 90.6 us
    pallas_call x1, Pallas kernels: 99.1 us -> 90.6 us  [shards(): pl.pallas_call(sparse_ring, out_shape=(flow, jax.ShapeDtypeStruct((1, LAN...]
    unnamed x1 -> x3, local copies, waits for them, and re-layouts: 1.67 us -> 2.34 us
where the time goes in v3:
time: 94.5 us; the launch traced here: 94.3 us
  Pallas kernels  90.6 us (96%)
  local copies, waits for them, and re-layouts  2.34 us (2%)
  between operations  1.37 us (1%)
    pallas_call x1, Pallas kernels, shards(): pl.pallas_call(sparse_ring, out_shape=(flow, jax.ShapeDtypeStruct((1, LAN...  90.6 us
    unnamed x3, local copies, waits for them, and re-layouts  2.34 us

profile of v3, /device:TPU:1, one launch (start us, length us, event | category | flops | bytes accessed | tf_op | source)
XLA Modules:
  0.0 94.3 jit_solution(3620402051122076541)
XLA Ops:
  1.3 90.6 %shard_map.93 = (f32[256,256]{1,0:T(8,128)}, s32[1,128]{1,0:T(1,128)}) custom-call(bf16[4,128,128]{2,1,0:T(8,128)(2,1)} %bitcast.10, s32[4]{0:T(128)} %bitcast.12, s32[4]{0:T(128)} %bitcast.14, s32[1,1,1]{2,1,0:T(1,128)S(6)} %copy.15.acount_hbm, bf16[12,128,128]{2,1,0:T(8,128)(2,1)} %bitcast.8, s32[12]{0:T(128)} %bitcast.16, s32[12]{0:T(128)} %bitcast.18, ...), custom_call_target="tpu_custom_call" | custom-call | tf_op jit(solution)/shard_map/pallas_call | solution.py:686
  91.9 0.0 copy-start
  91.9 0.7 copy-done
  92.6 1.7 %copy.17 = f32[256,256]{1,0:T(8,128)} copy(f32[256,256]{1,0:T(8,128)} %get-tuple-element.40) | data formatting | bytes 524288
  (1 shorter events, 0.0 us)
Async XLA Ops:
  91.9 0.7 copy-start

commit v4 on v3

--- a/solution.py
+++ b/solution.py
@@ -27,6 +27,8 @@
 PER_ROUND = 1
 ROUNDS = 26
 LAG = 3
+PIECES = (8,) + (2,) * 9
+FARTHEST = sorted(range(1, N_ROW), key=lambda k: -min(k, N_ROW - k))
 OWN = 1
 NEAR = OWN + NZB
 FRESH = NEAR + 2 * NZB
@@ -273,7 +275,7 @@
      abuf, lhs, a_notes, b_notes, needs, table, table_s, plan, plan_s, places, places_s,
      store, stage, landing, flag_note, flags, depth_note, depth_flags,
      acc, rs1, rs2, colsum, masses,
-     local_sem, hop_send, hop_recv, round_send, round_recv, a_send, a_recv, an_send, an_recv,
+     local_sem, plan_sem, hop_send, hop_recv, round_send, round_recv, a_send, a_recv, an_send, an_recv,
      bn_send, bn_recv, n_send, n_recv, f_send, f_recv, g_send, g_recv,
      d1_send, d1_recv, d2_send, d2_recv, m_send, m_recv) = scratch
     row = lax.axis_index("row")
@@ -321,15 +323,18 @@
         b_line = jnp.where(wide == row * PITCH + t, value, b_line)
     b_note[...] = b_line
     b_notes[row] = b_line
-    here = wide // (2 * PITCH) == col
-    odd = (wide // PITCH) % 2
-    a_line = jnp.full((1, IDS), -5000, jnp.int32)
+    a_rows_line = jnp.zeros((1, IDS), jnp.int32)
+    a_line = jnp.full((1, LANES), -5000, jnp.int32)
+    lane = lax.broadcasted_iota(jnp.int32, (1, LANES), 1)
     for s in range(NZA):
-        value = jnp.where(s < acount_s[0, 0, 0], acol_s[s] * COLB, -5000)
-        a_line = jnp.where((wide >= s * COLB) & (wide < (s + 1) * COLB), value + wide - s * COLB, a_line)
-        a_line = jnp.where(wide == NZA * COLB + s, arow_s[s], a_line)
-        a_note[s:s + 1, :] = jnp.where(here, value - odd * (KBT * COLB), -5000)
-    a_note[NZA:, :] = jnp.broadcast_to(a_line, (8 - NZA, IDS))
+        live = s < acount_s[0, 0, 0]
+        spot_at = jnp.where(live, col * KT + acol_s[s], -1)
+        a_rows_line = jnp.where(wide == spot_at, 1, a_rows_line)
+        value = jnp.where(live, acol_s[s] * COLB, -5000)
+        a_line = jnp.where((lane >= s * COLB) & (lane < (s + 1) * COLB), value + lane - s * COLB, a_line)
+        a_line = jnp.where(lane == NZA * COLB + s, arow_s[s], a_line)
+    a_note[:, :IDS] = a_rows_line
+    a_note[:, IDS:] = a_line
     a_notes[col] = a_note[...]
     pl.semaphore_wait(barrier, N_ROW - 1 + N_COL - 1 + N_DEPTH - 1)
 
@@ -380,43 +385,31 @@
 
     for k in range(1, N_COL):
         a_note_copy(k).start()
-    for k in range(1, N_ROW):
+    for k in FARTHEST:
         b_note_copy(k).start()
 
+    for k in range(1, N_COL):
+        a_note_copy(k).wait_recv()
+    need = a_notes[0][:, :IDS]
+    for c in range(1, N_COL):
+        need = jnp.maximum(need, a_notes[c][:, :IDS])
+    need_note[...] = need
+    needs[row] = need
+    for k in FARTHEST:
+        need_copy(k).start()
+    for way in (RIGHT, LEFT):
+        hop(way).start()
+    for k in range(1, N_COL):
+        a_copy(k).start()
+
     for k in range(1, N_ROW):
         b_note_copy(k).wait_recv()
-    for k in range(1, N_COL):
-        a_note_copy(k).wait_recv()
     blocks = b_notes[0]
     for r in range(1, N_ROW):
         blocks = jnp.maximum(blocks, b_notes[r])
-    wants = a_notes[0]
-    for c in range(1, N_COL):
-        wants = jnp.maximum(wants, a_notes[c])
-    gap = blocks - wants[:NZA, :]
-    hit = jnp.where((gap >= 0) & (gap < COLB), 1, 0)
-    need = jnp.max(hit, axis=0, keepdims=True)
-    need_note[...] = need
-    needs[row] = need
-    for k in range(1, N_ROW):
-        need_copy(k).start()
-    for way in (RIGHT, LEFT):
-        hop(way).start()
-    for k in range(1, N_COL):
-        a_copy(k).start()
-
-    lane = lax.broadcasted_iota(jnp.int32, (1, LANES), 1)
-    for c in range(N_COL):
-        left = a_notes[c][NZA:NZA + 1, :LANES]
-        slot = jnp.full((1, LANES), PITCH - 1, jnp.int32)
-        for h in range(2):
-            for t in range(NZB):
-                at = (2 * c + h) * PITCH + t
-                slot = jnp.where(left == blocks[:, at:at + 1] + h * (KBT * COLB), at, slot)
-        table[c] = jnp.where(lane < NZA * COLB, slot, left)
-    move = pltpu.make_async_copy(table, table_s, local_sem.at[2])
-    move.start()
-
+    inner = jnp.where(blocks >= 0, (wide // PITCH) * KBT + blocks // COLB, -1)
+    at_row = lax.broadcasted_iota(jnp.int32, (IDS, IDS), 0)
+    spread = jnp.where(at_row == inner, 1.0, 0.0).astype(jnp.bfloat16)
     z = lax.broadcasted_iota(jnp.int32, (N_ROW, IDS), 0)
     ident = lax.broadcasted_iota(jnp.int32, (N_ROW, IDS), 1)
     origin, spot = ident // PITCH, ident % PITCH
@@ -424,10 +417,11 @@
     reach = (jnp.where(spot < HALF, FAR, FAR - 1), jnp.where(spot < HALF, FAR - 1, FAR))
     for k in range(1, N_ROW):
         need_copy(k).wait_recv()
-    wanted = jnp.concatenate([needs[r] for r in range(N_ROW)], axis=0)
+    asked = jnp.concatenate([needs[r] for r in range(N_ROW)], axis=0)
+    wanted = jnp.dot(asked.astype(jnp.float32).astype(jnp.bfloat16), spread, preferred_element_type=jnp.float32)
     left_to_go, where_at = [], []
     for way in (RIGHT, LEFT):
-        inside = (wanted > 0) & (apart[way] >= 1) & (apart[way] <= reach[way])
+        inside = (wanted > 0.5) & (apart[way] >= 1) & (apart[way] <= reach[way])
         last = jnp.max(jnp.where(inside, apart[way], 0), axis=0, keepdims=True)
         left_to_go.append(jnp.where(apart[way] == 1, jnp.maximum(last - 1, 0), 0))
         where_at.append(jnp.where((apart[way] == 1) & (spot < NZB), NEAR + way * NZB + spot, 0))
@@ -461,59 +455,73 @@
             state[4 + way] = chosen
         return tuple(state)
 
-    state = lax.fori_loop(0, ROUNDS, one_round, (*left_to_go, *where_at, zero_plan, zero_plan, *waiting))
-    plan[RIGHT] = state[4]
-    plan[LEFT] = state[5]
-    plan_move = pltpu.make_async_copy(plan, plan_s, local_sem.at[10])
-    plan_move.start()
-    own_at = jnp.where((apart[0] == 0) & (spot < NZB), OWN + spot, 0)
-    final = jnp.maximum(jnp.maximum(state[2], state[3]), own_at)
-    places[0] = final[:, :LANES]
-    places[1] = final[:, LANES:]
-    places_move = pltpu.make_async_copy(places, places_s, local_sem.at[11])
-    places_move.start()
-    undone = jnp.maximum(state[0], state[1])
-    for late in state[6:]:
-        undone = jnp.maximum(undone, late)
-    undone = jnp.max(undone, axis=0, keepdims=True)
-    undone = jnp.maximum(undone[:, :LANES], undone[:, LANES:])
-    flag_note[...] = undone
-    flags[col] = undone
+    def plan_move(piece):
+        return pltpu.make_async_copy(plan.at[piece], plan_s.at[piece], plan_sem.at[piece])
+
+    def schedule(piece, first, last, state):
+        state = lax.fori_loop(first, last, one_round, (*state[:4], zero_plan, zero_plan, *state[6:]))
+        plan[piece, RIGHT] = state[4]
+        plan[piece, LEFT] = state[5]
+        plan_move(piece).start()
+        return state
+
+    state = schedule(0, 0, PIECES[0], (*left_to_go, *where_at, zero_plan, zero_plan, *waiting))
     own_b.wait()
     own_a.wait()
     own_keep.wait()
     for way in (RIGHT, LEFT):
         hop(way).wait_recv()
-    plan_move.wait()
-
-    def middle(k):
-        if k == 0:
-            for i in range(1, N_COL):
-                flag_copy(i).start()
-        if k == 8:
-            move.wait()
-            for i in range(1, N_COL):
-                a_copy(i).wait_recv()
-
-        if 8 <= k < 8 + N_COL:
-            for c in (k - 8,):
-                for s in range(NZA):
-                    block = abuf[c, s]
-                    which = table_s[c, 0, NZA * COLB + s]
-                    for i in range(ROWB):
-                        lhs[c, i * BS:(i + 1) * BS, s * BS:(s + 1) * BS] = jnp.where(
-                            which == i, block, jnp.zeros_like(block))
-        if k == 18:
-            for i in range(1, N_COL):
-                flag_copy(i).wait_recv()
-            total = flags[0]
-            for c in range(1, N_COL):
-                total = jnp.maximum(total, flags[c])
-            depth_note[...] = total
-            depth_flags[depth] = total
-            for i in range(1, N_DEPTH):
-                depth_flag_copy(i).start()
-
+
+    def finish_schedule(state):
+        own_at = jnp.where((apart[0] == 0) & (spot < NZB), OWN + spot, 0)
+        final = jnp.maximum(jnp.maximum(state[2], state[3]), own_at)
+        places[0] = final[:, :LANES]
+        places[1] = final[:, LANES:]
+        places_move.start()
+        undone = jnp.maximum(state[0], state[1])
+        for late in state[6:]:
+            undone = jnp.maximum(undone, late)
+        undone = jnp.max(undone, axis=0, keepdims=True)
+        undone = jnp.maximum(undone[:, :LANES], undone[:, LANES:])
+        flag_note[...] = undone
+        flags[col] = undone
+        for i in range(1, N_COL):
+            flag_copy(i).start()
+
+    def build_table():
+        for c in range(N_COL):
+            left = a_notes[c][:, IDS:]
+            slot = jnp.full((1, LANES), PITCH - 1, jnp.int32)
+            for h in range(2):
+                for t in range(NZB):
+                    at = (2 * c + h) * PITCH + t
+                    slot = jnp.where(left == blocks[:, at:at + 1] + h * (KBT * COLB), at, slot)
+            table[c] = jnp.where(lane < NZA * COLB, slot, left)
+        move.start()
+
+    def build_left(c):
+        for s in range(NZA):
+            block = abuf[c, s]
+            which = table_s[c, 0, NZA * COLB + s]
+            for i in range(ROWB):
+                lhs[c, i * BS:(i + 1) * BS, s * BS:(s + 1) * BS] = jnp.where(
+                    which == i, block, jnp.zeros_like(block))
+
+    def share_flag():
+        for i in range(1, N_COL):
+            flag_copy(i).wait_recv()
+        total = flags[0]
+        for c in range(1, N_COL):
+            total = jnp.maximum(total, flags[c])
+        depth_note[...] = total
+        depth_flags[depth] = total
+        for i in range(1, N_DEPTH):
+            depth_flag_copy(i).start()
+
+    move = pltpu.make_async_copy(table, table_s, local_sem.at[2])
+    places_move = pltpu.make_async_copy(places, places_s, local_sem.at[11])
+    piece_of = [p for p, n in enumerate(PIECES) for _ in range(n)]
+    starts = [sum(PIECES[:p]) for p in range(len(PIECES))]
     for k in range(ROUNDS + LAG):
         for way in (RIGHT, LEFT):
             if k >= LAG:
@@ -521,14 +529,29 @@
                 for m in range(PER_ROUND):
                     at = FRESH + (way * ROUNDS + k - LAG) * PER_ROUND + m
                     store[at] = landing[way, k - LAG, m]
+            if k < ROUNDS and way == RIGHT and k in starts:
+                plan_move(piece_of[k]).wait()
             if k < ROUNDS:
                 for m in range(PER_ROUND):
-                    stage[way, k, m] = store[plan_s[way, row, k * PER_ROUND + m]]
+                    stage[way, k, m] = store[plan_s[piece_of[k], way, row, k * PER_ROUND + m]]
                 round_copy(way, k).start()
-        middle(k)
+        if k + 1 < len(PIECES):
+            state = schedule(k + 1, starts[k + 1], starts[k + 1] + PIECES[k + 1], state)
+        if k + 1 == len(PIECES):
+            finish_schedule(state)
+        if k == len(PIECES):
+            build_table()
+        if k == len(PIECES) + 2:
+            move.wait()
+            for i in range(1, N_COL):
+                a_copy(i).wait_recv()
+        if len(PIECES) + 2 <= k < len(PIECES) + 2 + N_COL:
+            build_left(k - len(PIECES) - 2)
+        if k == len(PIECES) + 2 + N_COL:
+            share_flag()
     places_move.wait()
 
-    def part(j, carry):
+    def part(j):
         for c in range(N_COL):
             strips = []
             for s in range(NZA):
@@ -538,9 +561,7 @@
                     pair.append(store[places_s[at // LANES, row, at % LANES]])
                 strips.append(jnp.concatenate(pair, axis=1))
             acc[j] += jnp.dot(lhs[c], jnp.concatenate(strips, axis=0), preferred_element_type=jnp.float32)
-        return carry
-
-    lax.fori_loop(0, N_DEPTH, part, 0)
+
 
     def to_sibling(slot, half):
         part = pl.ds(half * BS, BS)
@@ -557,24 +578,29 @@
             send_sem=d2_send.at[half], recv_sem=d2_recv.at[half],
             device_id={"depth": across}, device_id_type=MESH)
 
-    for slot in range(2):
-        for half in range(ROWB):
-            to_sibling(slot, half).start()
+    part(across_sibling)
     for half in range(ROWB):
-        part = pl.ds(half * BS, BS)
+        to_sibling(0, half).start()
+    part(across)
+    for half in range(ROWB):
+        span = pl.ds(half * BS, BS)
         to_sibling(0, half).wait_recv()
-        acc[across, part] += rs1[0, part]
+        acc[across, span] += rs1[0, span]
         to_across(half).start()
+    part(sibling)
+    for half in range(ROWB):
+        to_sibling(1, half).start()
+    part(depth)
     total = jnp.zeros((1, QUARTER), jnp.float32)
     for half in range(ROWB):
-        part = pl.ds(half * BS, BS)
+        span = pl.ds(half * BS, BS)
         to_sibling(1, half).wait_recv()
-        mine = acc[depth, part] + rs1[1, part]
+        mine = acc[depth, span] + rs1[1, span]
         to_across(half).wait_recv()
-        product = mine + rs2[part]
+        product = mine + rs2[span]
         pruned = jnp.where(keep_ref[half:half + 1, :] > 0, product, 0.0)
         squares = pruned * pruned
-        flow_ref[part] = squares
+        flow_ref[span] = squares
         total = total + jnp.sum(squares, axis=0, keepdims=True)
     colsum[...] = total
     masses[row] = total
@@ -584,7 +610,7 @@
             src_ref=colsum, dst_ref=masses.at[row], send_sem=m_send.at[k], recv_sem=m_recv.at[k],
             device_id={"row": row_peer(k)}, device_id_type=MESH)
 
-    for k in range(1, N_ROW):
+    for k in FARTHEST:
         mass_copy(k).start()
     for k in range(1, N_ROW):
         mass_copy(k).wait_recv()
@@ -690,19 +716,19 @@
         out_specs=(vmem, vmem),
         scratch_shapes=words
         + [
-            pltpu.VMEM((8, IDS), jnp.int32),
+            pltpu.VMEM((1, IDS + LANES), jnp.int32),
             pltpu.VMEM((1, IDS), jnp.int32),
             pltpu.VMEM((1, IDS), jnp.int32),
         ]
         + left
         + [
-            pltpu.VMEM((N_COL, 8, IDS), jnp.int32),
+            pltpu.VMEM((N_COL, 1, IDS + LANES), jnp.int32),
             pltpu.VMEM((N_ROW, 1, IDS), jnp.int32),
             pltpu.VMEM((N_ROW, 1, IDS), jnp.int32),
             pltpu.VMEM((N_COL, 1, LANES), jnp.int32),
             pltpu.SMEM((N_COL, 1, LANES), jnp.int32),
-            pltpu.VMEM((2, N_ROW, LANES), jnp.int32),
-            pltpu.SMEM((2, N_ROW, LANES), jnp.int32),
+            pltpu.VMEM((len(PIECES), 2, N_ROW, LANES), jnp.int32),
+            pltpu.SMEM((len(PIECES), 2, N_ROW, LANES), jnp.int32),
             pltpu.VMEM((2, N_ROW, LANES), jnp.int32),
             pltpu.SMEM((2, N_ROW, LANES), jnp.int32),
             pltpu.VMEM((HELD, BS, BS), jnp.bfloat16),
@@ -714,7 +740,7 @@
             pltpu.VMEM((N_DEPTH, 1, LANES), jnp.int32),
         ]
         + sums
-        + [dma((12,))]
+        + [dma((12,)), dma((len(PIECES),))]
         + [dma((2,))] * 2
         + [dma((2, ROUNDS))] * 2
         + [dma((N_COL,))] * 4

time: 94.5 us -> 87 us (0.921)
  Pallas kernels: 90.6 us -> 82.8 us
    pallas_call x1, Pallas kernels: 90.6 us -> 82.8 us  [shards(): pl.pallas_call(sparse_ring, out_shape=(flow, jax.ShapeDtypeStruct((1, LAN...]
where the time goes in v4:
time: 87 us; the launch traced here: 86.7 us
  Pallas kernels  82.8 us (95%)
  local copies, waits for them, and re-layouts  2.34 us (3%)
  between operations  1.37 us (2%)
    pallas_call x1, Pallas kernels, shards(): pl.pallas_call(sparse_ring, out_shape=(flow, jax.ShapeDtypeStruct((1, LAN...  82.8 us
    unnamed x3, local copies, waits for them, and re-layouts  2.34 us

profile of v4, /device:TPU:1, one launch (start us, length us, event | category | flops | bytes accessed | tf_op | source)
XLA Modules:
  0.0 86.7 jit_solution(15754325613456617314)
XLA Ops:
  1.3 82.8 %shard_map.93 = (f32[256,256]{1,0:T(8,128)}, s32[1,128]{1,0:T(1,128)}) custom-call(bf16[4,128,128]{2,1,0:T(8,128)(2,1)} %bitcast.10, s32[4]{0:T(128)} %bitcast.12, s32[4]{0:T(128)} %bitcast.14, s32[1,1,1]{2,1,0:T(1,128)S(6)} %copy.15.acount_hbm, bf16[12,128,128]{2,1,0:T(8,128)(2,1)} %bitcast.8, s32[12]{0:T(128)} %bitcast.16, s32[12]{0:T(128)} %bitcast.18, ...), custom_call_target="tpu_custom_call" | custom-call | tf_op jit(solution)/shard_map/pallas_call | solution.py:712
  84.1 0.0 copy-start
  84.1 0.7 copy-done
  84.8 0.2 conditional.1
  85.0 1.7 %copy.17 = f32[256,256]{1,0:T(8,128)} copy(f32[256,256]{1,0:T(8,128)} %get-tuple-element.40) | data formatting | bytes 524288
Async XLA Ops:
  84.1 0.7 copy-start

commit v5 on v4

--- a/solution.py
+++ b/solution.py
@@ -25,9 +25,9 @@
 PITCH = 16
 IDS = N_ROW * PITCH
 PER_ROUND = 1
-ROUNDS = 26
+ROUNDS = 25
 LAG = 3
-PIECES = (8,) + (2,) * 9
+PIECES = (7,) + (2,) * 9
 FARTHEST = sorted(range(1, N_ROW), key=lambda k: -min(k, N_ROW - k))
 OWN = 1
 NEAR = OWN + NZB
@@ -622,7 +622,7 @@
     over = depth_flags[0]
     for i in range(1, N_DEPTH):
         over = jnp.maximum(over, depth_flags[i])
-    over_ref[...] = jnp.broadcast_to(jnp.max(over, axis=1, keepdims=True), (1, LANES))
+    over_ref[0, 0] = jnp.max(over)
 
     for way in (RIGHT, LEFT):
         hop(way).wait_send()
@@ -711,9 +711,9 @@
 
     result, over = pl.pallas_call(
         sparse_ring,
-        out_shape=(flow, jax.ShapeDtypeStruct((1, LANES), jnp.int32)),
+        out_shape=(flow, jax.ShapeDtypeStruct((1, 1), jnp.int32)),
         in_specs=[hbm] * 9,
-        out_specs=(vmem, vmem),
+        out_specs=(vmem, pl.BlockSpec(memory_space=pltpu.SMEM)),
         scratch_shapes=words
         + [
             pltpu.VMEM((1, IDS + LANES), jnp.int32),

time: 87 us -> 86.1 us (0.990)
  Pallas kernels: 82.8 us -> 81.8 us
    pallas_call x1, Pallas kernels: 82.8 us -> 81.8 us  [shards(): pl.pallas_call(sparse_ring, out_shape=(flow, jax.ShapeDtypeStruct((1, 1),...]
    unnamed x3 -> x1, local copies, waits for them, and re-layouts: 2.34 us -> 1.67 us
where the time goes in v5:
time: 86.1 us; the launch traced here: 85.7 us
  Pallas kernels  81.8 us (95%)
  between operations  2 us (2%)
  local copies, waits for them, and re-layouts  1.67 us (2%)
    pallas_call x1, Pallas kernels, shards(): pl.pallas_call(sparse_ring, out_shape=(flow, jax.ShapeDtypeStruct((1, 1),...  81.8 us

profile of v5, /device:TPU:1, one launch (start us, length us, event | category | flops | bytes accessed | tf_op | source)
XLA Modules:
  0.0 85.7 jit_solution(4231497194454267082)
XLA Ops:
  1.3 81.8 %shard_map.93 = (f32[256,256]{1,0:T(8,128)}, s32[1,1]{1,0:T(1,128)}) custom-call(bf16[4,128,128]{2,1,0:T(8,128)(2,1)} %bitcast.9, s32[4]{0:T(128)} %bitcast.11, s32[4]{0:T(128)} %bitcast.13, s32[1,1,1]{2,1,0:T(1,128)S(6)} %copy.15.acount_hbm, bf16[12,128,128]{2,1,0:T(8,128)(2,1)} %bitcast.7, s32[12]{0:T(128)} %bitcast.15, s32[12]{0:T(128)} %bitcast.17, ...), custom_call_target="tpu_custom_call" | custom-call | tf_op jit(solution)/shard_map/pallas_call | solution.py:712
  83.8 0.2 conditional.1
  84.0 1.7 %copy.17 = f32[256,256]{1,0:T(8,128)} copy(f32[256,256]{1,0:T(8,128)} %get-tuple-element.40) | data formatting | bytes 524288

commit v6 on v5

--- a/solution.py
+++ b/solution.py
@@ -296,7 +296,7 @@
         return lax.rem(depth + k, N_DEPTH)
 
     barrier = pltpu.get_barrier_semaphore()
-    for k in range(1, N_ROW):
+    for k in FARTHEST:
         pl.semaphore_signal(barrier, inc=1, device_id={"row": row_peer(k)}, device_id_type=MESH)
     for k in range(1, N_COL):
         pl.semaphore_signal(barrier, inc=1, device_id={"col": col_peer(k)}, device_id_type=MESH)

time: 86.1 us -> 86 us (level)
  no operation moved by 1% of the time
where the time goes in v6:
time: 86 us; the launch traced here: 85.6 us
  Pallas kernels  81.8 us (95%)
  between operations  2 us (2%)
  local copies, waits for them, and re-layouts  1.67 us (2%)
    pallas_call x1, Pallas kernels, shards(): pl.pallas_call(sparse_ring, out_shape=(flow, jax.ShapeDtypeStruct((1, 1),...  81.8 us

profile of v6, /device:TPU:1, one launch (start us, length us, event | category | flops | bytes accessed | tf_op | source)
XLA Modules:
  0.0 85.6 jit_solution(9046262840480815935)
XLA Ops:
  1.3 81.8 %shard_map.93 = (f32[256,256]{1,0:T(8,128)}, s32[1,1]{1,0:T(1,128)}) custom-call(bf16[4,128,128]{2,1,0:T(8,128)(2,1)} %bitcast.9, s32[4]{0:T(128)} %bitcast.11, s32[4]{0:T(128)} %bitcast.13, s32[1,1,1]{2,1,0:T(1,128)S(6)} %copy.15.acount_hbm, bf16[12,128,128]{2,1,0:T(8,128)(2,1)} %bitcast.7, s32[12]{0:T(128)} %bitcast.15, s32[12]{0:T(128)} %bitcast.17, ...), custom_call_target="tpu_custom_call" | custom-call | tf_op jit(solution)/shard_map/pallas_call | solution.py:712
  83.8 0.2 conditional.1
  84.0 1.7 %copy.17 = f32[256,256]{1,0:T(8,128)} copy(f32[256,256]{1,0:T(8,128)} %get-tuple-element.40) | data formatting | bytes 524288
